TPU v7x, 32 devices: a whole 2x2x4 slice. The times are simulated.
32 devices in a mesh: row: 4 (over y, x), col: 8 (over z, core).
Axes of the slice: x: 2, y: 2, z: 4, core: 2. Of those that a mesh axis runs over, the one named last changes fastest.
Arguments:
- inputs: bfloat16 [2048, 25600], P('row', 'col'), may hold values from -6 to 6
- out_grads: bfloat16 [2048, 5120], P('col', 'row'), may hold values from -0.125 to 0.125
- weights: bfloat16 [5120, 25600], P('row', 'col'), may hold values from -3 to 3
- momentum: float32 [5120, 25600], P('row', 'col'), may hold values from -13 to 13
- right_factor: float32 [25600, 256], P('col'), may hold values from -6 to 6
Outputs:
- weights_new: float32 [5120, 25600], P('row', 'col')
- momentum_new: float32 [5120, 25600], P('row', 'col')
- factor_new: float32 [25600, 256], P('col')
All inputs are finite; a program needn't handle non-finite values.
Results may differ from a plain program's by a relative error of at most 0.0003.
Values may be sent and summed in bfloat16 or wider, within the bound.
No kernel may reach another device: no remote copies, remote signals or barrier semaphores. Data moves between devices by JAX's collectives and lax.ppermute only.
A program may use at most 128 MiB of HBM per device.

v0:
```python
import math
import jax
import jax.numpy as jnp
from jax import lax
from jax.sharding import PartitionSpec as P

M = 5120
N = 25600
RANK = 256
mix_rate = 0.95
step_rate = 0.3
weight_decay = 0.1
tiny_eps = 1e-06
highest = lax.Precision.HIGHEST


def inner_rows(left_side, right_in):
    return lax.dot_general(left_side, right_in, (((0,), (0,)), ((), ())), precision=highest)


def orthonormal(sketch_rows, gram_total):
    factor_low = jnp.linalg.cholesky(gram_total)
    return jax.scipy.linalg.solve_triangular(factor_low, sketch_rows.T, lower=True).T


def on_device(inputs, out_grads, weights, momentum, right_factor):
    grads_all = lax.all_gather(out_grads, "col", axis=0, tiled=True)
    gradient = lax.dot_general(
        grads_all,
        lax.all_gather(inputs, "row", axis=0, tiled=True),
        (((0,), (0,)), ((), ())),
        preferred_element_type=jnp.float32,
    )
    moment = momentum + gradient
    sketch_part = jnp.dot(moment, right_factor, precision=highest)
    sketch_rows = lax.psum(sketch_part, "col")
    gram_total = lax.psum(inner_rows(sketch_rows, sketch_rows), "row")
    basis_rows = orthonormal(sketch_rows, gram_total)
    right_part = inner_rows(moment, basis_rows)
    right_share = lax.psum_scatter(right_part, "row", scatter_dimension=0, tiled=True)
    squares = lax.psum(jnp.sum(right_share * right_share, axis=0), ("row", "col"))
    right_side = lax.all_gather(right_share, "row", axis=0, tiled=True)
    column_scale = lax.rsqrt(squares / N + tiny_eps)
    factor_new = right_side * column_scale
    momentum_new = moment - (1.0 - mix_rate) * jnp.dot(basis_rows, right_side.T, precision=highest)
    update = jnp.dot(basis_rows, factor_new.T, precision=highest)
    weights_new = (
        weights.astype(jnp.float32) * (1.0 - step_rate * weight_decay)
        - step_rate * math.sqrt(M / RANK) * update
    )
    return (weights_new, momentum_new, factor_new)


def solution(mesh):
    placed = (P("row", "col"), P("col", "row"), P("row", "col"), P("row", "col"), P("col", None))
    return jax.shard_map(
        on_device,
        mesh=mesh,
        in_specs=placed,
        out_specs=(P("row", "col"), P("row", "col"), P("col", None)),
        check_vma=False,
    )
```

profile of v0, /device:TPU:0, one launch (start us, length us, event | category | flops | bytes accessed | tf_op | source)
XLA Modules:
  0.0 616.2 jit_solution(3706774686516627048)
XLA Ops:
  7.2 0.0 copy-start
  7.2 0.0 all-gather.4.cloned.1.call-start
  7.2 0.7 all-gather.4.cloned.1.call-update
  7.9 0.0 all-gather.6.cloned.1.call-start
  8.0 0.7 all-gather.6.cloned.1.call-update
  8.7 0.0 all-reduce.4.cloned.1.call-start
  8.7 59.7 %all-gather.4.cloned.1.call-done = bf16[2048,1280]{1,0:T(8,128)(2,1)} async-done(((bf16[256,1280]{1,0:T(8,128)(2,1)}), bf16[2048,1280]{1,0:T(8,128)(2,1)}) %all-gather.4.cloned.1.call-update) | async-done | bytes 5242896 | tf_op jit(solution)/shard_map/all_gather | solution.py:27
  68.4 127.4 %all-gather.6.cloned.1.call-done = bf16[2048,3200]{1,0:T(8,128)(2,1)} async-done(((bf16[512,3200]{1,0:T(8,128)(2,1)}), bf16[2048,3200]{1,0:T(8,128)(2,1)}) %all-gather.6.cloned.1.call-update) | async-done | bytes 13107216 | tf_op jit(solution)/shard_map/all_gather | solution.py:30
  195.8 29.4 %convolution_add_fusion = f32[1280,3200]{1,0:T(8,128)} fusion(f32[1280,3200]{1,0:T(8,128)} %param.8, bf16[2048,1280]{1,0:T(8,128)(2,1)} %all-gather.4.cloned.1.call-done, bf16[2048,3200]{1,0:T(8,128)(2,1)} %all-gather.6.cloned.1.call-done), kind=kOutput, calls=%fused_computation.2 | convolution fusion | flops 16781312000 | bytes 51118080 | tf_op jit(solution)/shard_map/dot_general | solution.py:28
  225.1 0.0 copy-done
  225.1 17.8 %fusion.15 = f32[1280,256]{1,0:T(8,128)} fusion(f32[1280,3200]{1,0:T(8,128)} %convolution_add_fusion, f32[3200,256]{1,0:T(8,128)S(1)} %copy-done), kind=kOutput, calls=%fused_computation.41 | convolution fusion | flops 12582912000 | bytes 20971520 | tf_op jit(solution)/shard_map/dot_general | solution.py:35
  242.9 0.0 all-reduce.4.cloned.1.call-update
  242.9 0.0 all-reduce.6.cloned.1.call-start
  243.0 60.5 %all-reduce.4.cloned.1.call-done = f32[1280,256]{1,0:T(8,128)} async-done(((f32[1280,256]{1,0:T(8,128)}), f32[1280,256]{1,0:T(8,128)}) %all-reduce.4.cloned.1.call-update) | async-done | bytes 1310736 | tf_op jit(solution)/shard_map/psum | solution.py:36
  303.5 0.0 copy-start.5
  303.5 4.8 fusion.16
  308.3 0.0 all-reduce.6.cloned.1.call-update
  308.4 0.2 reduce-scatter.2.cloned.1.call-start
  308.6 42.0 %all-reduce.6.cloned.1.call-done = f32[256,256]{0,1:T(8,128)} async-done(((f32[256,256]{0,1:T(8,128)}), f32[256,256]{0,1:T(8,128)}) %all-reduce.6.cloned.1.call-update) | async-done | bytes 262160 | tf_op jit(solution)/shard_map/psum | solution.py:37
  350.6 1.1 copy.9
  351.7 1.0 fusion.5
  352.7 11.7 %cholesky.50 = f32[128,128]{1,0:T(8,128)S(1)} custom-call(f32[128,128]{1,0:T(8,128)S(1)} %cholesky.118), custom_call_target="Cholesky" | custom-call | tf_op jit(solution)/shard_map/jit(cholesky)/cholesky | solution.py:22
  364.4 9.8 %custom-call.15 = f32[1,128,128]{1,2,0:T(8,128)S(1)} custom-call(f32[1,128,128]{2,1,0:T(8,128)S(1)} %get-tuple-element.24), custom_call_target="InvertDiagBlocksLowerTriangular" | custom-call | tf_op jit(solution)/shard_map/jit(cholesky)/cholesky | solution.py:22
  374.3 0.2 constant_dynamic-update-slice_fusion.1
  374.5 0.3 convolution_subtract_fusion.1
  374.8 11.7 %cholesky.105 = f32[128,128]{1,0:T(8,128)S(1)} custom-call(f32[128,128]{1,0:T(8,128)S(1)} %convolution_subtract_fusion.1), custom_call_target="Cholesky" | custom-call | tf_op jit(solution)/shard_map/jit(cholesky)/cholesky | solution.py:22
  386.5 0.7 compare_reduce_fusion
  388.6 0.1 triangular_solve.57
  388.6 4.2 while.1
  388.8 0.6 fusion.31
  389.4 1.4 bitcast_dynamic-update-slice_fusion.2
  390.8 0.6 fusion.31
  391.4 1.4 bitcast_dynamic-update-slice_fusion.2
  392.8 19.7 %custom-call.16 = f32[2,128,128]{1,2,0:T(8,128)S(1)} custom-call(f32[2,128,128]{2,1,0:T(8,128)S(1)} %get-tuple-element.10), custom_call_target="InvertDiagBlocksLowerTriangular" | custom-call | tf_op jit(solution)/shard_map/jit(_solve_triangular)/triangular_solve | solution.py:23
  412.5 0.0 copy-done.5
  412.5 0.8 fusion.3
  413.3 0.0 copy-start.2
  413.3 1.2 convolution_subtract_fusion
  414.5 0.8 fusion.7
  415.2 0.0 copy-start.6
  415.2 32.1 %fusion.2 = f32[3200,256]{1,0:T(8,128)} fusion(f32[1280,3200]{1,0:T(8,128)} %convolution_add_fusion, f32[128,1280]{1,0:T(8,128)S(1)} %fusion.7, f32[128,1280]{1,0:T(8,128)S(1)} %fusion.3), kind=kOutput, calls=%fused_computation.11 | convolution fusion | flops 12583239680 | bytes 20971520 | tf_op jit(solution)/shard_map/dot_general | solution.py:18
  447.4 0.0 reduce-scatter.2.cloned.1.call-update
  447.4 0.0 all-gather.8.cloned.1.call-start
  447.4 45.1 %reduce-scatter.2.cloned.1.call-done = f32[800,256]{1,0:T(8,128)} async-done(((f32[3200,256]{1,0:T(8,128)}), f32[800,256]{1,0:T(8,128)}) %reduce-scatter.2.cloned.1.call-update) | async-done | bytes 819216 | tf_op jit(solution)/shard_map/reduce_scatter | solution.py:40
  492.5 0.0 all-gather.8.cloned.1.call-update
  492.6 1.3 multiply_reduce_fusion
  493.8 40.3 %psum.23 = f32[256]{0:T(256)S(1)} all-reduce(f32[256]{0:T(256)S(1)} %multiply_reduce_fusion), channel_id=1, replica_groups=mesh['row'=4,'col'=8] {'row','col'}, use_global_device_ids=true, to_apply=%region_8.9 | all-reduce | flops 256 | bytes 2048 | tf_op jit(solution)/shard_map/psum | solution.py:41
  534.1 6.0 all-gather.8.cloned.1.call-done
  540.1 2.1 broadcast_multiply_fusion
  542.2 0.0 copy-done.2
  542.2 0.0 copy-done.6
  542.2 0.0 copy-start.3
  542.3 0.0 copy-start.4
  542.3 32.8 %fusion.1 = f32[1280,3200]{1,0:T(8,128)} fusion(f32[3200,256]{1,0:T(8,128)S(1)} %broadcast_multiply_fusion, bf16[1280,3200]{1,0:T(8,128)(2,1)} %param.7, f32[128,1280]{1,0:T(8,128)S(1)} %fusion.7, f32[128,1280]{1,0:T(8,128)S(1)} %fusion.3), kind=kOutput, calls=%fused_computation.6 | convolution fusion | flops 12599623680 | bytes 29163520 | tf_op jit(solution)/shard_map/dot_general | solution.py:46
  575.0 0.0 copy-done.3
  575.0 0.0 copy-done.4
  575.0 0.0 copy-start.1
  575.0 34.1 %fusion = f32[1280,3200]{1,0:T(8,128)} fusion(f32[1280,3200]{1,0:T(8,128)} %convolution_add_fusion, f32[3200,256]{1,0:T(8,128)S(1)} %copy-done.4, f32[128,1280]{1,0:T(8,128)} %copy-done.6, f32[128,1280]{1,0:T(8,128)} %copy-done.2), kind=kOutput, calls=%fused_computation.4 | convolution fusion | flops 12591431680 | bytes 37355520 | tf_op jit(solution)/shard_map/dot_general | solution.py:45
  609.1 0.0 copy-done.1
  (10 shorter events, 0.2 us)
Async XLA Ops:
  7.2 217.9 %copy-start = (f32[3200,256]{1,0:T(8,128)S(1)}, f32[3200,256]{1,0:T(8,128)}, u32[]{:S(2)}) copy-start(f32[3200,256]{1,0:T(8,128)} %param.9) | copy-start | bytes 9830404
  7.2 61.2 %all-gather.4.cloned.1.call-start = ((), (), s32[]{:S(2)}) async-start(), calls=%async_computation.1 | async-start | bytes 5898240 | tf_op jit(solution)/shard_map/all_gather | solution.py:27
  7.9 187.8 %all-gather.6.cloned.1.call-start = ((), (), s32[]{:S(2)}) async-start(), calls=%async_computation.2 | async-start | bytes 16384000 | tf_op jit(solution)/shard_map/all_gather | solution.py:30
  8.7 294.8 %all-reduce.4.cloned.1.call-start = ((), (), s32[]{:S(2)}) async-start(), calls=%async_computation.3 | async-start | bytes 2621440 | tf_op jit(solution)/shard_map/psum | solution.py:36
  242.9 107.7 %all-reduce.6.cloned.1.call-start = ((), (), s32[]{:S(2)}) async-start(), calls=%async_computation.4 | async-start | bytes 524288 | tf_op jit(solution)/shard_map/psum | solution.py:37
  303.5 109.0 %copy-start.5 = (f32[1280,256]{1,0:T(8,128)S(1)}, f32[1280,256]{1,0:T(8,128)}, u32[]{:S(2)}) copy-start(f32[1280,256]{1,0:T(8,128)} %all-reduce.4.cloned.1.call-done) | copy-start | bytes 3932164
  308.4 184.2 %reduce-scatter.2.cloned.1.call-start = ((), (), s32[]{:S(2)}) async-start(), calls=%async_computation.5 | async-start | bytes 4096000 | tf_op jit(solution)/shard_map/reduce_scatter | solution.py:40
  413.3 129.0 %copy-start.2 = (f32[128,1280]{1,0:T(8,128)}, f32[128,1280]{1,0:T(8,128)S(1)}, u32[]{:S(2)}) copy-start(f32[128,1280]{1,0:T(8,128)S(1)} %fusion.3) | copy-start | bytes 1966084
  415.2 127.0 %copy-start.6 = (f32[128,1280]{1,0:T(8,128)}, f32[128,1280]{1,0:T(8,128)S(1)}, u32[]{:S(2)}) copy-start(f32[128,1280]{1,0:T(8,128)S(1)} %fusion.7) | copy-start | bytes 1966084
  447.4 92.7 %all-gather.8.cloned.1.call-start = ((), (), s32[]{:S(2)}) async-start(), calls=%async_computation.6 | async-start | bytes 4096000 | tf_op jit(solution)/shard_map/all_gather | solution.py:42
  542.2 32.8 %copy-start.3 = (f32[3200,256]{1,0:T(8,128)}, f32[3200,256]{1,0:T(8,128)S(1)}, u32[]{:S(2)}) copy-start(f32[3200,256]{1,0:T(8,128)S(1)} %broadcast_multiply_fusion) | copy-start | bytes 9830404
  542.3 32.8 %copy-start.4 = (f32[3200,256]{1,0:T(8,128)S(1)}, f32[3200,256]{1,0:T(8,128)}, u32[]{:S(2)}) copy-start(f32[3200,256]{1,0:T(8,128)} %all-gather.8.cloned.1.call-done) | copy-start | bytes 9830404
  575.0 34.1 %copy-start.1 = (f32[3200,256]{1,0:T(8,128)S(1)}, f32[3200,256]{1,0:T(8,128)}, u32[]{:S(2)}) copy-start(f32[3200,256]{1,0:T(8,128)} %param.9) | copy-start | bytes 9830404
Sparse Core Ops, SparseCore 0:
  9.6 58.6 all-gather.3
  70.2 125.5 all-gather.5
  243.0 60.4 all-reduce.3
  308.5 42.0 all-reduce.5
  447.5 44.9 reduce-scatter.1
  494.2 45.7 all-gather.7
where the time goes:
time: 623 us; the launch traced here: 616 us
  waiting for transfers between devices  342 us (55%)
  matrix products  154 us (25%)
  other arithmetic  58.1 us (9%)
  blocking collectives  40.3 us (6%)
  between operations  15.8 us (3%)
    all_gather x1, waiting for transfers between devices, on_device(): lax.all_gather(inputs, 'row', axis=0, tiled=True)  127 us
    psum x1, waiting for transfers between devices, on_device(): sketch_rows = lax.psum(sketch_part, 'col')  60.5 us
    all_gather x1, waiting for transfers between devices, on_device(): grads_all = lax.all_gather(out_grads, 'col', axis=0, tiled=True)  59.7 us
    reduce_scatter x1, waiting for transfers between devices, on_device(): lax.psum_scatter(right_part, 'row', scatter_dimension=0, tiled=True)  45.1 us
    psum x1, waiting for transfers between devices, on_device(): gram_total = lax.psum(inner_rows(sketch_rows, sketch_rows), 'row')  42 us
    psum x1, blocking collectives, on_device(): lax.psum(jnp.sum(right_share * right_share, axis=0), ('row', 'col'))  40.3 us
    dot_general x2, matrix products, inner_rows(): lax.dot_general(left_side, right_in, (((0,), (0,)), ((), ())), precision=...  36.9 us
    dot_general x1, matrix products, on_device(): jnp.dot(basis_rows, right_side.T, precision=highest)  34.1 us
  transfers between devices with their start and end apart: 6, of which 6 were waited for; matrix products, arithmetic and copies ran while one was open for 0% of the time, Pallas kernels for 0%

commit v1 on v0

--- a/solution.py
+++ b/solution.py
@@ -3,6 +3,7 @@
 import jax.numpy as jnp
 from jax import lax
 from jax.sharding import PartitionSpec as P
+from jax.lax import axis_index, axis_size, ppermute
 
 M = 5120
 N = 25600
@@ -24,7 +25,16 @@
 
 
 def on_device(inputs, out_grads, weights, momentum, right_factor):
-    grads_all = lax.all_gather(out_grads, "col", axis=0, tiled=True)
+    lanes = axis_size("col")
+    last = sorted(((dev_i, (dev_i + 1) % lanes) for dev_i in range(lanes)))
+    y2 = out_grads
+    arrivals = [y2]
+    for jj in range(1, lanes):
+        y2 = ppermute(y2, "col", perm=last)
+        arrivals.insert(0, y2)
+    piece_now = jnp.concatenate(arrivals, axis=0)
+    vec_out = axis_index("col") + 1
+    grads_all = jnp.roll(piece_now, vec_out * out_grads.shape[0], axis=0)
     gradient = lax.dot_general(
         grads_all,
         lax.all_gather(inputs, "row", axis=0, tiled=True),

time: 623 us -> 581 us (0.933)
  waiting for transfers between devices: 342 us -> 256 us
  local copies, waits for them, and re-layouts: 5.14 us -> 34.3 us
  matrix products: 154 us -> 167 us
    all_gather x1, waiting for transfers between devices: 127 us -> 17.9 us  [on_device(): lax.all_gather(inputs, 'row', axis=0, tiled=True)]
    ppermute x0 -> x7, waiting for transfers between devices: none -> 83.7 us  [on_device(): y2 = ppermute(y2, 'col', perm=last)]
    all_gather x1 -> x0, waiting for transfers between devices: 59.7 us -> none  [on_device(): grads_all = lax.all_gather(out_grads, 'col', axis=0, tiled=True)]
    unnamed x14 -> x49, local copies, waits for them, and re-layouts: 0.04 us -> 28.3 us
    dot_general x1, matrix products: 17.8 us -> 28.8 us  [on_device(): sketch_part = jnp.dot(moment, right_factor, precision=highest)]
  transfers between devices with their start and end apart: 6 -> 12, of which waited for: 6 -> 12; matrix products, arithmetic and copies ran while one was open for 0% -> 5% of each run, Pallas kernels for 0% -> 0%
where the time goes in v1:
time: 581 us; the launch traced here: 573 us
  waiting for transfers between devices  256 us (44%)
  matrix products  167 us (29%)
  other arithmetic  58.1 us (10%)
  blocking collectives  40.3 us (7%)
  local copies, waits for them, and re-layouts  34.3 us (6%)
  between operations  15.5 us (3%)
    ppermute x7, waiting for transfers between devices, on_device(): y2 = ppermute(y2, 'col', perm=last)  83.7 us
    psum x1, waiting for transfers between devices, on_device(): sketch_rows = lax.psum(sketch_part, 'col')  60.5 us
    reduce_scatter x1, waiting for transfers between devices, on_device(): lax.psum_scatter(right_part, 'row', scatter_dimension=0, tiled=True)  45.1 us
    psum x1, waiting for transfers between devices, on_device(): gram_total = lax.psum(inner_rows(sketch_rows, sketch_rows), 'row')  42.2 us
    psum x1, blocking collectives, on_device(): lax.psum(jnp.sum(right_share * right_share, axis=0), ('row', 'col'))  40.3 us
    dot_general x2, matrix products, inner_rows(): lax.dot_general(left_side, right_in, (((0,), (0,)), ((), ())), precision=...  36.5 us
    dot_general x1, matrix products, on_device(): jnp.dot(basis_rows, right_side.T, precision=highest)  34.2 us
    another operation x6, other arithmetic, orthonormal(): factor_low = jnp.linalg.cholesky(gram_total)  33.9 us
  transfers between devices with their start and end apart: 12, of which 12 were waited for; matrix products, arithmetic and copies ran while one was open for 5% of the time, Pallas kernels for 0%

profile of v1, /device:TPU:0, one launch (start us, length us, event | category | flops | bytes accessed | tf_op | source)
XLA Modules:
  0.0 572.6 jit_solution(720878356198002838)
XLA Ops:
  7.2 0.7 all-gather.3.cloned.1.call-update
  8.0 0.5 collective-permute-start
  8.5 12.5 %collective-permute-done = bf16[256,1280]{1,0:T(8,128)(2,1)S(1)} collective-permute-done((bf16[256,1280]{1,0:T(8,128)(2,1)}, bf16[256,1280]{1,0:T(8,128)(2,1)S(1)}, u32[]{:S(2)}, u32[]{:S(2)}) %collective-permute-start) | collective-permute-done | bytes 655392 | tf_op jit(solution)/shard_map/ppermute | solution.py:33
  21.0 0.9 copy-done.7
  21.9 11.8 %collective-permute-done.1 = bf16[256,1280]{1,0:T(8,128)(2,1)S(1)} collective-permute-done((bf16[256,1280]{1,0:T(8,128)(2,1)S(1)}, bf16[256,1280]{1,0:T(8,128)(2,1)S(1)}, u32[]{:S(2)}, u32[]{:S(2)}) %collective-permute-start.1) | collective-permute-done | bytes 655392 | tf_op jit(solution)/shard_map/ppermute | solution.py:33
  33.7 0.9 copy-done.9
  34.5 11.8 %collective-permute-done.2 = bf16[256,1280]{1,0:T(8,128)(2,1)S(1)} collective-permute-done((bf16[256,1280]{1,0:T(8,128)(2,1)S(1)}, bf16[256,1280]{1,0:T(8,128)(2,1)S(1)}, u32[]{:S(2)}, u32[]{:S(2)}) %collective-permute-start.2) | collective-permute-done | bytes 655392 | tf_op jit(solution)/shard_map/ppermute | solution.py:33
  46.3 0.9 copy-done.11
  47.2 11.8 %collective-permute-done.3 = bf16[256,1280]{1,0:T(8,128)(2,1)S(1)} collective-permute-done((bf16[256,1280]{1,0:T(8,128)(2,1)S(1)}, bf16[256,1280]{1,0:T(8,128)(2,1)S(1)}, u32[]{:S(2)}, u32[]{:S(2)}) %collective-permute-start.3) | collective-permute-done | bytes 655392 | tf_op jit(solution)/shard_map/ppermute | solution.py:33
  59.0 0.8 copy-done.13
  59.8 11.8 %collective-permute-done.4 = bf16[256,1280]{1,0:T(8,128)(2,1)S(1)} collective-permute-done((bf16[256,1280]{1,0:T(8,128)(2,1)S(1)}, bf16[256,1280]{1,0:T(8,128)(2,1)S(1)}, u32[]{:S(2)}, u32[]{:S(2)}) %collective-permute-start.4) | collective-permute-done | bytes 655392 | tf_op jit(solution)/shard_map/ppermute | solution.py:33
  71.7 0.8 copy-done.15
  72.5 11.9 %collective-permute-done.5 = bf16[256,1280]{1,0:T(8,128)(2,1)} collective-permute-done((bf16[256,1280]{1,0:T(8,128)(2,1)S(1)}, bf16[256,1280]{1,0:T(8,128)(2,1)}, u32[]{:S(2)}, u32[]{:S(2)}) %collective-permute-start.5) | collective-permute-done | bytes 655392 | tf_op jit(solution)/shard_map/ppermute | solution.py:33
  84.4 12.1 %collective-permute-done.6 = bf16[256,1280]{1,0:T(8,128)(2,1)} collective-permute-done((bf16[256,1280]{1,0:T(8,128)(2,1)}, bf16[256,1280]{1,0:T(8,128)(2,1)}, u32[]{:S(2)}, u32[]{:S(2)}) %collective-permute-start.6) | collective-permute-done | bytes 655392 | tf_op jit(solution)/shard_map/ppermute | solution.py:33
  96.5 2.0 constant_dynamic-update-slice_fusion.15
  98.5 2.0 constant_dynamic-update-slice_fusion.14
  100.5 2.0 constant_dynamic-update-slice_fusion.13
  102.4 2.0 constant_dynamic-update-slice_fusion.12
  104.4 2.0 constant_dynamic-update-slice_fusion.11
  106.4 2.0 constant_dynamic-update-slice_fusion.10
  108.3 2.0 constant_dynamic-update-slice_fusion.9
  110.3 2.0 constant_dynamic-update-slice_fusion.8
  112.2 2.0 constant_dynamic-update-slice_fusion.7
  114.2 2.0 constant_dynamic-update-slice_fusion.6
  116.2 0.9 constant_dynamic-update-slice_fusion.5
  117.1 0.9 constant_dynamic-update-slice_fusion.4
  117.9 0.9 constant_dynamic-update-slice_fusion.3
  118.8 0.9 constant_dynamic-update-slice_fusion.2
  119.7 0.9 constant_dynamic-update-slice_fusion.1
  120.6 0.9 constant_dynamic-update-slice_fusion
  121.5 17.9 %all-gather.3.cloned.1.call-done = bf16[2048,3200]{1,0:T(8,128)(2,1)} async-done(((bf16[512,3200]{1,0:T(8,128)(2,1)}), bf16[2048,3200]{1,0:T(8,128)(2,1)}) %all-gather.3.cloned.1.call-update) | async-done | bytes 13107216 | tf_op jit(solution)/shard_map/all_gather | solution.py:40
  139.3 29.4 %convolution_add_fusion = f32[1280,3200]{1,0:T(8,128)} fusion(f32[1280,3200]{1,0:T(8,128)} %param.8, bf16[2048,3200]{1,0:T(8,128)(2,1)} %all-gather.3.cloned.1.call-done, bf16[4096,1280]{1,0:T(8,128)(2,1)} %constant_dynamic-update-slice_fusion, s32[]{:T(128)S(6)} %select_n.18), kind=kOutput, calls=%fused_computation.2 | convolution fusion | flops 16781312000 | bytes 51118084 | tf_op jit(solution)/shard_map/dot_general | solution.py:38
  168.7 28.8 %fusion.17 = f32[1280,256]{1,0:T(8,128)} fusion(f32[1280,3200]{1,0:T(8,128)} %convolution_add_fusion, f32[3200,256]{1,0:T(8,128)S(1)} %copy-done), kind=kOutput, calls=%fused_computation.59 | convolution fusion | flops 12582912000 | bytes 20971520 | tf_op jit(solution)/shard_map/dot_general | solution.py:45
  197.5 0.0 all-reduce.6.cloned.1.call-start
  197.6 60.5 %all-reduce.4.cloned.1.call-done = f32[1280,256]{1,0:T(8,128)} async-done(((f32[1280,256]{1,0:T(8,128)}), f32[1280,256]{1,0:T(8,128)}) %all-reduce.4.cloned.1.call-update) | async-done | bytes 1310736 | tf_op jit(solution)/shard_map/psum | solution.py:46
  258.1 4.6 fusion.18
  262.9 42.2 %all-reduce.6.cloned.1.call-done = f32[256,256]{0,1:T(8,128)} async-done(((f32[256,256]{0,1:T(8,128)}), f32[256,256]{0,1:T(8,128)}) %all-reduce.6.cloned.1.call-update) | async-done | bytes 262160 | tf_op jit(solution)/shard_map/psum | solution.py:47
  305.0 1.1 copy.9
  306.1 1.0 fusion.6
  307.1 11.7 %cholesky.50 = f32[128,128]{1,0:T(8,128)S(1)} custom-call(f32[128,128]{1,0:T(8,128)S(1)} %cholesky.118), custom_call_target="Cholesky" | custom-call | tf_op jit(solution)/shard_map/jit(cholesky)/cholesky | solution.py:23
  318.9 9.8 %custom-call.15 = f32[1,128,128]{1,2,0:T(8,128)S(1)} custom-call(f32[1,128,128]{2,1,0:T(8,128)S(1)} %get-tuple-element.24), custom_call_target="InvertDiagBlocksLowerTriangular" | custom-call | tf_op jit(solution)/shard_map/jit(cholesky)/cholesky | solution.py:23
  328.7 0.2 constant_dynamic-update-slice_fusion.17
  328.9 0.3 convolution_subtract_fusion.1
  329.2 11.7 %cholesky.105 = f32[128,128]{1,0:T(8,128)S(1)} custom-call(f32[128,128]{1,0:T(8,128)S(1)} %convolution_subtract_fusion.1), custom_call_target="Cholesky" | custom-call | tf_op jit(solution)/shard_map/jit(cholesky)/cholesky | solution.py:23
  340.9 0.6 compare_reduce_fusion
  342.9 0.1 triangular_solve.57
  343.0 4.4 while.1
  343.4 0.6 fusion.32
  344.0 1.4 bitcast_dynamic-update-slice_fusion.2
  345.4 0.6 fusion.32
  346.0 1.4 bitcast_dynamic-update-slice_fusion.2
  347.4 19.7 %custom-call.16 = f32[2,128,128]{1,2,0:T(8,128)S(1)} custom-call(f32[2,128,128]{2,1,0:T(8,128)S(1)} %get-tuple-element.10), custom_call_target="InvertDiagBlocksLowerTriangular" | custom-call | tf_op jit(solution)/shard_map/jit(_solve_triangular)/triangular_solve | solution.py:24
  367.1 1.8 fusion.4
  368.9 2.5 convolution_subtract_fusion
  371.4 0.7 fusion.8
  372.2 31.8 %fusion.3 = f32[3200,256]{1,0:T(8,128)} fusion(f32[1280,3200]{1,0:T(8,128)} %convolution_add_fusion, f32[128,1280]{1,0:T(8,128)S(1)} %fusion.8, f32[128,1280]{1,0:T(8,128)S(1)} %fusion.4), kind=kOutput, calls=%fused_computation.12 | convolution fusion | flops 12583239680 | bytes 20971520 | tf_op jit(solution)/shard_map/dot_general | solution.py:19
  404.1 0.0 all-gather.5.cloned.1.call-start
  404.1 45.1 %reduce-scatter.2.cloned.1.call-done = f32[800,256]{1,0:T(8,128)} async-done(((f32[3200,256]{1,0:T(8,128)}), f32[800,256]{1,0:T(8,128)}) %reduce-scatter.2.cloned.1.call-update) | async-done | bytes 819216 | tf_op jit(solution)/shard_map/reduce_scatter | solution.py:50
  449.2 1.3 multiply_reduce_fusion
  450.5 40.3 %psum.23 = f32[256]{0:T(256)S(1)} all-reduce(f32[256]{0:T(256)S(1)} %multiply_reduce_fusion), channel_id=1, replica_groups=mesh['row'=4,'col'=8] {'row','col'}, use_global_device_ids=true, to_apply=%region_8.9 | all-reduce | flops 256 | bytes 2048 | tf_op jit(solution)/shard_map/psum | solution.py:51
  490.8 5.9 %all-gather.5.cloned.1.call-done = f32[3200,256]{1,0:T(8,128)} async-done(((f32[800,256]{1,0:T(8,128)}), f32[3200,256]{1,0:T(8,128)}) %all-gather.5.cloned.1.call-update) | async-done | bytes 3276816 | tf_op jit(solution)/shard_map/all_gather | solution.py:52
  496.7 2.1 broadcast_multiply_fusion
  498.9 32.8 %fusion.1 = f32[1280,3200]{1,0:T(8,128)} fusion(f32[3200,256]{1,0:T(8,128)S(1)} %broadcast_multiply_fusion, bf16[1280,3200]{1,0:T(8,128)(2,1)} %param.7, f32[128,1280]{1,0:T(8,128)S(1)} %fusion.8, f32[128,1280]{1,0:T(8,128)S(1)} %fusion.4), kind=kOutput, calls=%fused_computation.6 | convolution fusion | flops 12599623680 | bytes 29163520 | tf_op jit(solution)/shard_map/dot_general | solution.py:56
  531.7 34.2 %fusion = f32[1280,3200]{1,0:T(8,128)} fusion(f32[1280,3200]{1,0:T(8,128)} %convolution_add_fusion, f32[3200,256]{1,0:T(8,128)S(1)} %copy-done.4, f32[128,1280]{1,0:T(8,128)} %copy-done.5, f32[128,1280]{1,0:T(8,128)} %copy-done.2), kind=kOutput, calls=%fused_computation.4 | convolution fusion | flops 12591431680 | bytes 37355520 | tf_op jit(solution)/shard_map/dot_general | solution.py:55
  (52 shorter events, 0.4 us)
Async XLA Ops:
  7.2 161.5 %copy-start = (f32[3200,256]{1,0:T(8,128)S(1)}, f32[3200,256]{1,0:T(8,128)}, u32[]{:S(2)}) copy-start(f32[3200,256]{1,0:T(8,128)} %param.9) | copy-start | bytes 9830404
  7.2 132.2 %all-gather.3.cloned.1.call-start = ((), (), s32[]{:S(2)}) async-start(), calls=%async_computation.1 | async-start | bytes 16384000 | tf_op jit(solution)/shard_map/all_gather | solution.py:40
  7.9 250.2 %all-reduce.4.cloned.1.call-start = ((), (), s32[]{:S(2)}) async-start(), calls=%async_computation.2 | async-start | bytes 2621440 | tf_op jit(solution)/shard_map/psum | solution.py:46
  8.0 13.1 %collective-permute-start = (bf16[256,1280]{1,0:T(8,128)(2,1)}, bf16[256,1280]{1,0:T(8,128)(2,1)S(1)}, u32[]{:S(2)}, u32[]{:S(2)}) collective-permute-start(bf16[256,1280]{1,0:T(8,128)(2,1)} %param.6), channel_id=1, source_target_pairs={{0,1},{1,2},{2,3},{3,4},{4,5},{5,6},{6,7},{7,0},{8,9},{9,10},{10,1... | collective-permute-start | bytes 1966088 | tf_op jit(solution)/shard_map/ppermute | solution.py:33
  21.0 0.9 copy-start.7
  21.9 11.8 %collective-permute-start.1 = (bf16[256,1280]{1,0:T(8,128)(2,1)S(1)}, bf16[256,1280]{1,0:T(8,128)(2,1)S(1)}, u32[]{:S(2)}, u32[]{:S(2)}) collective-permute-start(bf16[256,1280]{1,0:T(8,128)(2,1)S(1)} %collective-permute-done), channel_id=1, source_target_pairs={{0,1},{1,2},{2,3},{3,4},{4,5},{5,6},{6,7},{7,0},{8,9},{9,10},{10,1... | collective-permute-start | bytes 1966088 | tf_op jit(solution)/shard_map/ppermute | solution.py:33
  33.7 0.9 copy-start.9
  34.5 11.8 %collective-permute-start.2 = (bf16[256,1280]{1,0:T(8,128)(2,1)S(1)}, bf16[256,1280]{1,0:T(8,128)(2,1)S(1)}, u32[]{:S(2)}, u32[]{:S(2)}) collective-permute-start(bf16[256,1280]{1,0:T(8,128)(2,1)S(1)} %collective-permute-done.1), channel_id=1, source_target_pairs={{0,1},{1,2},{2,3},{3,4},{4,5},{5,6},{6,7},{7,0},{8,9},{9,10},{10,1... | collective-permute-start | bytes 1966088 | tf_op jit(solution)/shard_map/ppermute | solution.py:33
  46.3 0.9 copy-start.11
  47.2 11.8 %collective-permute-start.3 = (bf16[256,1280]{1,0:T(8,128)(2,1)S(1)}, bf16[256,1280]{1,0:T(8,128)(2,1)S(1)}, u32[]{:S(2)}, u32[]{:S(2)}) collective-permute-start(bf16[256,1280]{1,0:T(8,128)(2,1)S(1)} %collective-permute-done.2), channel_id=1, source_target_pairs={{0,1},{1,2},{2,3},{3,4},{4,5},{5,6},{6,7},{7,0},{8,9},{9,10},{10,1... | collective-permute-start | bytes 1966088 | tf_op jit(solution)/shard_map/ppermute | solution.py:33
  59.0 0.8 copy-start.13
  59.8 11.8 %collective-permute-start.4 = (bf16[256,1280]{1,0:T(8,128)(2,1)S(1)}, bf16[256,1280]{1,0:T(8,128)(2,1)S(1)}, u32[]{:S(2)}, u32[]{:S(2)}) collective-permute-start(bf16[256,1280]{1,0:T(8,128)(2,1)S(1)} %collective-permute-done.3), channel_id=1, source_target_pairs={{0,1},{1,2},{2,3},{3,4},{4,5},{5,6},{6,7},{7,0},{8,9},{9,10},{10,1... | collective-permute-start | bytes 1966088 | tf_op jit(solution)/shard_map/ppermute | solution.py:33
  71.7 0.8 copy-start.15
  72.5 11.9 %collective-permute-start.5 = (bf16[256,1280]{1,0:T(8,128)(2,1)S(1)}, bf16[256,1280]{1,0:T(8,128)(2,1)}, u32[]{:S(2)}, u32[]{:S(2)}) collective-permute-start(bf16[256,1280]{1,0:T(8,128)(2,1)S(1)} %collective-permute-done.4), channel_id=1, source_target_pairs={{0,1},{1,2},{2,3},{3,4},{4,5},{5,6},{6,7},{7,0},{8,9},{9,10},{10,1... | collective-permute-start | bytes 1966088 | tf_op jit(solution)/shard_map/ppermute | solution.py:33
  84.4 12.1 %collective-permute-start.6 = (bf16[256,1280]{1,0:T(8,128)(2,1)}, bf16[256,1280]{1,0:T(8,128)(2,1)}, u32[]{:S(2)}, u32[]{:S(2)}) collective-permute-start(bf16[256,1280]{1,0:T(8,128)(2,1)} %collective-permute-done.5), channel_id=1, source_target_pairs={{0,1},{1,2},{2,3},{3,4},{4,5},{5,6},{6,7},{7,0},{8,9},{9,10},{10,1... | collective-permute-start | bytes 1966088 | tf_op jit(solution)/shard_map/ppermute | solution.py:33
  84.4 31.8 %copy-start.16 = (bf16[256,1280]{1,0:T(8,128)(2,1)S(1)}, bf16[256,1280]{1,0:T(8,128)(2,1)}, u32[]{:S(2)}) copy-start(bf16[256,1280]{1,0:T(8,128)(2,1)} %copy-done.15) | copy-start | bytes 1966084
  84.4 32.7 %copy-start.14 = (bf16[256,1280]{1,0:T(8,128)(2,1)S(1)}, bf16[256,1280]{1,0:T(8,128)(2,1)}, u32[]{:S(2)}) copy-start(bf16[256,1280]{1,0:T(8,128)(2,1)} %copy-done.13) | copy-start | bytes 1966084
  84.4 33.5 %copy-start.12 = (bf16[256,1280]{1,0:T(8,128)(2,1)S(1)}, bf16[256,1280]{1,0:T(8,128)(2,1)}, u32[]{:S(2)}) copy-start(bf16[256,1280]{1,0:T(8,128)(2,1)} %copy-done.11) | copy-start | bytes 1966084
  84.4 34.4 %copy-start.10 = (bf16[256,1280]{1,0:T(8,128)(2,1)S(1)}, bf16[256,1280]{1,0:T(8,128)(2,1)}, u32[]{:S(2)}) copy-start(bf16[256,1280]{1,0:T(8,128)(2,1)} %copy-done.9) | copy-start | bytes 1966084
  84.4 35.3 %copy-start.8 = (bf16[256,1280]{1,0:T(8,128)(2,1)S(1)}, bf16[256,1280]{1,0:T(8,128)(2,1)}, u32[]{:S(2)}) copy-start(bf16[256,1280]{1,0:T(8,128)(2,1)} %copy-done.7) | copy-start | bytes 1966084
  84.4 36.2 %copy-start.6 = (bf16[256,1280]{1,0:T(8,128)(2,1)S(1)}, bf16[256,1280]{1,0:T(8,128)(2,1)}, u32[]{:S(2)}) copy-start(bf16[256,1280]{1,0:T(8,128)(2,1)} %param.6) | copy-start | bytes 1966084
  197.5 107.5 %all-reduce.6.cloned.1.call-start = ((), (), s32[]{:S(2)}) async-start(), calls=%async_computation.3 | async-start | bytes 524288 | tf_op jit(solution)/shard_map/psum | solution.py:47
  262.8 186.4 %reduce-scatter.2.cloned.1.call-start = ((), (), s32[]{:S(2)}) async-start(), calls=%async_computation.4 | async-start | bytes 4096000 | tf_op jit(solution)/shard_map/reduce_scatter | solution.py:50
  368.9 130.0 %copy-start.2 = (f32[128,1280]{1,0:T(8,128)}, f32[128,1280]{1,0:T(8,128)S(1)}, u32[]{:S(2)}) copy-start(f32[128,1280]{1,0:T(8,128)S(1)} %fusion.4) | copy-start | bytes 1966084
  372.2 126.7 %copy-start.5 = (f32[128,1280]{1,0:T(8,128)}, f32[128,1280]{1,0:T(8,128)S(1)}, u32[]{:S(2)}) copy-start(f32[128,1280]{1,0:T(8,128)S(1)} %fusion.8) | copy-start | bytes 1966084
  404.1 92.7 %all-gather.5.cloned.1.call-start = ((), (), s32[]{:S(2)}) async-start(), calls=%async_computation.5 | async-start | bytes 4096000 | tf_op jit(solution)/shard_map/all_gather | solution.py:52
  498.9 32.8 %copy-start.3 = (f32[3200,256]{1,0:T(8,128)}, f32[3200,256]{1,0:T(8,128)S(1)}, u32[]{:S(2)}) copy-start(f32[3200,256]{1,0:T(8,128)S(1)} %broadcast_multiply_fusion) | copy-start | bytes 9830404
  498.9 32.8 %copy-start.4 = (f32[3200,256]{1,0:T(8,128)S(1)}, f32[3200,256]{1,0:T(8,128)}, u32[]{:S(2)}) copy-start(f32[3200,256]{1,0:T(8,128)} %all-gather.5.cloned.1.call-done) | copy-start | bytes 9830404
  531.7 34.2 %copy-start.1 = (f32[3200,256]{1,0:T(8,128)S(1)}, f32[3200,256]{1,0:T(8,128)}, u32[]{:S(2)}) copy-start(f32[3200,256]{1,0:T(8,128)} %param.9) | copy-start | bytes 9830404
Sparse Core Ops, SparseCore 0:
  9.8 129.4 all-gather.2
  197.7 60.4 all-reduce.3
  262.9 42.0 all-reduce.5
  404.2 44.9 reduce-scatter.1
  450.9 45.7 all-gather.4
